TPU v7x, 128 devices: a whole 4x4x4 slice. The times are simulated.
128 devices in a mesh: dp: 32 (over x, z, core), enc: 4 (over y).
Axes of the slice: x: 4, y: 4, z: 4, core: 2. Of those that a mesh axis runs over, the one named last changes fastest.
Arguments:
- hidden: bfloat16 [16384, 4096], P('dp', 'enc'), may hold values from -6 to 6
- norm_gain: float32 [4096], replicated, may hold values from 0.25 to 1.75
- w_query: bfloat16 [4096, 2048], P('dp', 'enc'), may hold values from -0.09375 to 0.09375
- w_key: bfloat16 [896, 2048], P('dp', 'enc'), may hold values from -0.1875 to 0.1875
- w_value: bfloat16 [896, 2048], P('dp', 'enc'), may hold values from -0.1875 to 0.1875
- w_out: bfloat16 [2048, 4096], P('enc', 'dp'), may hold values from -0.125 to 0.125
- w_cond: bfloat16 [4096, 896], P('dp', 'enc'), may hold values from -0.75 to 0.75
- enc_gain: float32 [896], replicated, may hold values from 0.25 to 1.75
- store: bfloat16 [1024, 128, 896], P(('dp', 'enc')), may hold values from -6 to 6
- neighbour_ids: int32 [512], P(('dp', 'enc')), may hold values from 0 to 1023, as said below
- out_grad: bfloat16 [16384, 4096], P('dp', 'enc'), may hold values from -6 to 6
Outputs:
- layer_out: bfloat16 [16384, 4096], P('dp', 'enc')
- hidden_grad: float32 [16384, 4096], P('dp', 'enc')
- query_grad: float32 [4096, 2048], P('dp', 'enc')
- key_grad: float32 [896, 2048], P('dp', 'enc')
- value_grad: float32 [896, 2048], P('dp', 'enc')
- out_weight_grad: float32 [2048, 4096], P('enc', 'dp')
- cond_grad: float32 [4096, 896], P('dp', 'enc')
Inputs may be any that keep to these rules, and one draw needn't show every extreme that they name: `neighbour_ids`: slot n names a neighbour stored on a device of the same data index as the device holding slot n (device k holds rows k * 8 to (k + 1) * 8 - 1). Among the 4 slots of one device at most 2 name rows of one device, and for every data index one device is named by exactly 2 slots of each of the 4 devices.
All inputs are finite; a program needn't handle non-finite values.
Results may differ from a plain program's by a relative error of at most 0.019.
Values may be sent and summed in bfloat16 or wider, within the bound.
A program may use at most 192 MiB of HBM per device.

v0:
```python
import jax
import jax.numpy as jnp
from jax import lax
from jax.sharding import PartitionSpec as P

HSZ = 128
SPAN = 64
NBR = 2
NL = 128
epsilon = 1e-05


def side_by_side(arrays, axis, dim, along):
    ends, at = ([], 0)
    for a in arrays[:-1]:
        at += a.shape[along]
        ends.append(at)
    both = jnp.concatenate(arrays, axis=along)
    return tuple(jnp.split(lax.all_gather(both, axis, axis=dim, tiled=True), ends, axis=along))


def joined_along(tiles, dim):
    tiles = jnp.moveaxis(tiles, 0, dim)
    dims = tiles.shape
    return tiles.reshape(*dims[:dim], dims[dim] * dims[dim + 1], *dims[dim + 2 :])


def copy_for_each(shard, axis):
    copies = jnp.broadcast_to(shard, (lax.axis_size(axis), *shard.shape))
    return lax.all_to_all(copies, axis, split_axis=0, concat_axis=0, tiled=True)


def collect(shard, axis, dim):
    return joined_along(copy_for_each(shard, axis), dim)


def in_blocks(shard, dim, peers):
    dims = shard.shape
    tiles = shard.reshape(*dims[:dim], peers, dims[dim] // peers, *dims[dim + 1 :])
    return jnp.moveaxis(tiles, dim, 0)


def summed_on_arrival(shard, axis, dim):
    peers = lax.axis_size(axis)
    tiles = lax.all_to_all(in_blocks(shard, dim, peers), axis, 0, 0, tiled=True)
    return jnp.sum(tiles.astype(jnp.float32), axis=0)


def one_scatter(arrays, axis, dims):
    peers = lax.axis_size(axis)
    tiles = [in_blocks(a, dim, peers) for a, dim in zip(arrays, dims)]
    lines = jnp.concatenate([b.reshape(peers, -1) for b in tiles], axis=1)
    extent = max(16, -(-lines.shape[1] // 1024) * 8)
    lines = jnp.pad(lines, ((0, 0), (0, extent * 128 - lines.shape[1]))).reshape(-1, 128)
    flat, at, done = (lax.psum_scatter(lines, axis, tiled=True).reshape(-1), 0, [])
    for b in tiles:
        part = b[0]
        done.append(flat[at : at + part.size].reshape(part.shape))
        at += part.size
    return tuple(done)


def rms_scale(values):
    return lax.rsqrt(jnp.mean(values * values, axis=-1, keepdims=True) + epsilon)


def encoder_input(raw_rows, cond_rows):
    enc_in = raw_rows.astype(jnp.float32) + cond_rows.astype(jnp.float32)[..., None, :]
    return (enc_in, rms_scale(enc_in))


def encode_rows(raw_rows, cond_rows, enc_gain):
    enc_in, enc_rstd = encoder_input(raw_rows, cond_rows)
    return (enc_in * enc_rstd * enc_gain).astype(jnp.bfloat16)


def cond_gradient(raw_rows, cond_rows, enc_gain, grad_rows):
    enc_in, enc_rstd = encoder_input(raw_rows, cond_rows)
    scaled_enc = enc_gain * grad_rows.astype(jnp.float32)
    enc_mean = jnp.mean(enc_in * scaled_enc, axis=-1, keepdims=True)
    return jnp.sum(enc_rstd * scaled_enc - enc_in * enc_rstd**3 * enc_mean, axis=-2)


def contract_first(left, right):
    return lax.dot_general(
        left, right, (((0,), (0,)), ((), ())), preferred_element_type=jnp.float32
    )


def contract_last(left, right):
    return lax.dot_general(
        left, right, (((1,), (1,)), ((), ())), preferred_element_type=jnp.float32
    )


def shards(
    hidden,
    norm_gain,
    w_query,
    w_key,
    w_value,
    w_out,
    w_cond,
    enc_gain,
    store,
    neighbour_ids,
    out_grad,
):
    groups = lax.axis_size("enc")
    member = lax.axis_index("enc")
    tok_rows = hidden.shape[0]
    feature_cols = hidden.shape[1]
    model_width = feature_cols * groups
    head_cols = w_query.shape[1]
    enc_width = w_key.shape[0] * lax.axis_size("dp")
    enc_cols = w_cond.shape[1]
    span_count = tok_rows // SPAN
    requests = neighbour_ids.shape[0]
    capacity = max(2, (requests + 1) // 2)
    store_rows = store.shape[0]
    heads_here = head_cols // HSZ
    keys_len = NBR * NL
    score_scale = HSZ ** (-0.5)
    full_rows = lax.all_gather(hidden, "enc", axis=1, tiled=True)
    inputs = full_rows.astype(jnp.float32)
    row_rstd = rms_scale(inputs)
    normed = (inputs * row_rstd * norm_gain).astype(jnp.bfloat16)
    w_query_all, w_key_all, w_value_all, w_cond_all = (
        lax.all_gather(w_query, "dp", axis=0, tiled=True),
        *side_by_side((w_key, w_value), "dp", 0, 1),
        lax.all_gather(w_cond, "dp", axis=0, tiled=True),
    )
    queries = jnp.dot(normed, w_query_all, preferred_element_type=jnp.float32).astype(jnp.bfloat16)
    w_out_all = lax.all_gather(w_out, "dp", axis=1, tiled=True)
    summary = jnp.mean(inputs.reshape(span_count, SPAN, model_width), axis=1).astype(jnp.bfloat16)
    cond_part = jnp.dot(summary, w_cond_all, preferred_element_type=jnp.float32).astype(
        jnp.bfloat16
    )
    condition = collect(cond_part, "enc", 1)
    request_order = jnp.arange(requests)
    my_spans = (member * requests + request_order) // NBR
    cond_req = jnp.take(condition, my_spans, axis=0)
    owner_of = neighbour_ids // store_rows % groups
    store_row = neighbour_ids % store_rows
    earlier = (owner_of[:, None] == owner_of[None, :]) & (
        request_order[None, :] < request_order[:, None]
    )
    slot_rank = jnp.sum(earlier.astype(jnp.int32), axis=1)
    slot_index = owner_of * capacity + slot_rank
    selection = slot_index[None, :] == jnp.arange(groups * capacity)[:, None]
    row_buffer = jnp.sum(jnp.where(selection, store_row[None, :], 0), axis=1).reshape(
        groups, capacity
    )
    raw_buffer = lax.all_to_all(
        jnp.take(
            store,
            lax.all_to_all(row_buffer, "enc", split_axis=0, concat_axis=0, tiled=True),
            axis=0,
        ),
        "enc",
        split_axis=0,
        concat_axis=0,
        tiled=True,
    )
    raw_mine = jnp.take(raw_buffer.reshape(groups * capacity, NL, enc_width), slot_index, axis=0)
    encoded_mine = encode_rows(raw_mine, cond_req, enc_gain)
    encoded = lax.all_gather(encoded_mine, "enc", axis=0, tiled=True)
    flat_enc = encoded.reshape(-1, enc_width)
    keys_proj = jnp.dot(flat_enc, w_key_all, preferred_element_type=jnp.float32).astype(
        jnp.bfloat16
    )
    values_proj = jnp.dot(flat_enc, w_value_all, preferred_element_type=jnp.float32).astype(
        jnp.bfloat16
    )
    query_heads = queries.reshape(span_count, SPAN, heads_here, HSZ)
    key_heads = keys_proj.reshape(span_count, keys_len, heads_here, HSZ)
    value_heads = values_proj.reshape(span_count, keys_len, heads_here, HSZ)
    scores = (
        jnp.einsum("cqhd,ckhd->chqk", query_heads, key_heads, preferred_element_type=jnp.float32)
        * score_scale
    )
    attn_full = jax.nn.softmax(scores, axis=-1)
    attn_weights = attn_full.astype(jnp.bfloat16)
    attended = (
        jnp.einsum("chqk,ckhd->cqhd", attn_weights, value_heads, preferred_element_type=jnp.float32)
        .astype(jnp.bfloat16)
        .reshape(tok_rows, head_cols)
    )
    out_term = jnp.dot(attended, w_out_all, preferred_element_type=jnp.float32)
    projected = summed_on_arrival(out_term.astype(jnp.bfloat16), "enc", 1)
    layer_out = (hidden.astype(jnp.float32) + projected).astype(jnp.bfloat16)
    grad_rows = lax.all_gather(out_grad, "enc", axis=1, tiled=True)
    attended_grad = contract_last(grad_rows, w_out_all).astype(jnp.bfloat16)
    out_weight_grad = lax.psum_scatter(
        contract_first(attended, grad_rows).astype(jnp.bfloat16),
        "dp",
        scatter_dimension=1,
        tiled=True,
    ).astype(jnp.float32)
    grad_heads = attended_grad.reshape(span_count, SPAN, heads_here, HSZ)
    prob_grad = jnp.einsum(
        "cqhd,ckhd->chqk", grad_heads, value_heads, preferred_element_type=jnp.float32
    )
    score_grad = (
        attn_full
        * (prob_grad - jnp.sum(attn_full * prob_grad, axis=-1, keepdims=True))
        * score_scale
    ).astype(jnp.bfloat16)
    query_act_grad = (
        jnp.einsum("chqk,ckhd->cqhd", score_grad, key_heads, preferred_element_type=jnp.float32)
        .astype(jnp.bfloat16)
        .reshape(tok_rows, head_cols)
    )
    key_act_grad = (
        jnp.einsum("chqk,cqhd->ckhd", score_grad, query_heads, preferred_element_type=jnp.float32)
        .astype(jnp.bfloat16)
        .reshape(-1, head_cols)
    )
    value_act_grad = (
        jnp.einsum("chqk,cqhd->ckhd", attn_weights, grad_heads, preferred_element_type=jnp.float32)
        .astype(jnp.bfloat16)
        .reshape(-1, head_cols)
    )
    query_grad = lax.psum_scatter(
        contract_first(normed, query_act_grad).astype(jnp.bfloat16),
        "dp",
        scatter_dimension=0,
        tiled=True,
    ).astype(jnp.float32)
    enc_term = contract_last(key_act_grad, w_key_all) + contract_last(value_act_grad, w_value_all)
    encoded_grad = (
        summed_on_arrival(enc_term.astype(jnp.bfloat16), "enc", 0)
        .astype(jnp.bfloat16)
        .reshape(requests, NL, enc_width)
    )
    cond_mine = cond_gradient(raw_mine, cond_req, enc_gain, encoded_grad)
    slot_grads = collect(cond_mine, "enc", 0)
    cond_delta = jnp.sum(slot_grads.reshape(span_count, NBR, enc_width), axis=1).astype(
        jnp.bfloat16
    )
    delta_cols = lax.dynamic_slice_in_dim(cond_delta, member * enc_cols, enc_cols, 1)
    key_term = contract_first(flat_enc, key_act_grad)
    value_term = contract_first(flat_enc, value_act_grad)
    cond_term = contract_first(summary, delta_cols)
    key_grad, value_grad, cond_grad = tuple(
        (
            part.astype(jnp.float32)
            for part in one_scatter(
                (
                    key_term.astype(jnp.bfloat16),
                    value_term.astype(jnp.bfloat16),
                    cond_term.astype(jnp.bfloat16),
                ),
                "dp",
                (0, 0, 0),
            )
        )
    )
    summary_term = contract_last(delta_cols, w_cond_all)
    normed_term = contract_last(query_act_grad, w_query_all)
    normed_grad, summary_grad = (
        lax.psum(normed_term.astype(jnp.bfloat16), "enc").astype(jnp.float32),
        lax.psum(summary_term.astype(jnp.bfloat16), "enc").astype(jnp.float32),
    )
    scaled = normed_grad * norm_gain
    row_mean = jnp.mean(inputs * scaled, axis=-1, keepdims=True)
    full_grad = (
        grad_rows.astype(jnp.float32)
        + (row_rstd * scaled - inputs * row_rstd**3 * row_mean)
        + jnp.repeat(summary_grad / SPAN, SPAN, axis=0)
    )
    hidden_grad = lax.dynamic_slice_in_dim(full_grad, member * feature_cols, feature_cols, 1)
    return (layer_out, hidden_grad, query_grad, key_grad, value_grad, out_weight_grad, cond_grad)


def solution(mesh):
    placed = (
        P("dp", "enc"),
        P(),
        P("dp", "enc"),
        P("dp", "enc"),
        P("dp", "enc"),
        P("enc", "dp"),
        P("dp", "enc"),
        P(),
        P(("dp", "enc"), None, None),
        P(("dp", "enc")),
        P("dp", "enc"),
    )
    return jax.shard_map(
        shards,
        mesh=mesh,
        in_specs=placed,
        out_specs=(
            P("dp", "enc"),
            P("dp", "enc"),
            P("dp", "enc"),
            P("dp", "enc"),
            P("dp", "enc"),
            P("enc", "dp"),
            P("dp", "enc"),
        ),
        check_vma=False,
    )
```

profile of v0, /device:TPU:0, one launch (start us, length us, event | category | flops | bytes accessed | tf_op | source)
XLA Modules:
  0.0 741.9 jit_solution(10964547584921568469)
XLA Ops:
  11.8 9.6 %all_to_all.40 = s32[4,1,2]{2,1,0:T(1,128)S(1)} all-to-all(s32[4,1,2]{2,1,0:T(1,128)S(1)} %bitcast.99), channel_id=1, replica_groups=mesh['dp'=32,'enc'=4] {'enc'}, dimensions={0} | all-to-all | bytes 64 | tf_op jit(solution)/shard_map/all_to_all | solution.py:157
  23.8 3.1 broadcast_select_fusion
  26.9 3.6 all-to-all-start.1
  30.6 49.5 %all-gather.9.cloned.1.call-done = bf16[512,4096]{1,0:T(8,128)(2,1)} async-done(((bf16[512,1024]{1,0:T(8,128)(2,1)}), bf16[512,4096]{1,0:T(8,128)(2,1)}) %all-gather.9.cloned.1.call-update) | async-done | bytes 4194320 | tf_op jit(solution)/shard_map/all_gather | solution.py:124
  80.1 3.0 bitcast_reduce_fusion
  83.1 43.9 %all-gather.11.cloned.1.call-done = bf16[4096,224]{0,1:T(8,128)(2,1)} async-done(((bf16[128,224]{0,1:T(8,128)(2,1)}), bf16[4096,224]{0,1:T(8,128)(2,1)}) %all-gather.11.cloned.1.call-update) | async-done | bytes 1835024 | tf_op jit(solution)/shard_map/all_gather | solution.py:131
  129.8 4.3 all-to-all-start.2
  136.4 3.1 all-to-all-done.2
  144.0 29.2 %all-gather.21.cloned.1.call-done = bf16[32,28,1024]{2,1,0:T(8,128)(2,1)} async-done(((bf16[1,28,1024]{2,1,0:T(8,128)(2,1)}), bf16[32,28,1024]{2,1,0:T(8,128)(2,1)}) %all-gather.21.cloned.1.call-update) | async-done | bytes 1835024 | tf_op jit(solution)/shard_map/all_gather | solution.py:19
  173.2 3.7 reshape.330
  177.0 3.1 multiply_reduce_fusion.1
  180.6 40.4 %all-gather.15.cloned.1.call-done = bf16[4096,512]{1,0:T(8,128)(2,1)} async-done(((bf16[128,512]{1,0:T(8,128)(2,1)}), bf16[4096,512]{1,0:T(8,128)(2,1)}) %all-gather.15.cloned.1.call-update) | async-done | bytes 4194320 | tf_op jit(solution)/shard_map/all_gather | solution.py:129
  221.0 5.8 convolution_convert_fusion.11
  227.0 39.4 %all-gather.13.cloned.1.call-done = bf16[16,128,896]{2,1,0:T(8,128)(2,1)} async-done(((bf16[4,128,896]{2,1,0:T(8,128)(2,1)}), bf16[16,128,896]{2,1,0:T(8,128)(2,1)}) %all-gather.13.cloned.1.call-update) | async-done | bytes 3670032 | tf_op jit(solution)/shard_map/all_gather | solution.py:167
  266.4 5.9 convolution_convert_fusion.6
  272.3 4.0 reshape.289
  276.3 6.4 convolution_convert_fusion.7
  282.7 4.2 reshape.287
  291.4 6.0 fusion.34
  297.7 18.7 %all-gather.19.cloned.1.call-done = bf16[512,4096]{1,0:T(8,128)(2,1)} async-done(((bf16[512,1024]{1,0:T(8,128)(2,1)}), bf16[512,4096]{1,0:T(8,128)(2,1)}) %all-gather.19.cloned.1.call-update) | async-done | bytes 4194320 | tf_op jit(solution)/shard_map/all_gather | solution.py:192
  316.4 6.5 convolution_convert_fusion
  323.0 6.5 copy.112
  329.9 38.4 %all-gather.17.cloned.1.call-done = bf16[512,4096]{1,0:T(8,128)(2,1)} async-done(((bf16[512,128]{1,0:T(8,128)(2,1)}), bf16[512,4096]{1,0:T(8,128)(2,1)}) %all-gather.17.cloned.1.call-update) | async-done | bytes 4194320 | tf_op jit(solution)/shard_map/all_gather | solution.py:134
  368.4 5.8 convolution_convert_fusion.10
  374.3 3.8 fusion.9
  378.1 16.3 %fusion.37 = bf16[8,64,4,128]{3,1,2,0:T(8,128)(2,1)} fusion(bf16[8,256,4,128]{3,2,1,0:T(4,128)(2,1)} %reshape.289, f32[8,4,64,256]{3,2,1,0:T(8,128)} %fusion.9, f32[8,4,64,256]{3,2,1,0:T(8,128)} %get-tuple-element.50, f32[8,4,64]{2,1,0:T(4,128)S(1)} %get-tuple-element.49), kind=kOutput, calls=%fused_computation.62 | convolution fusion | flops 138152192 | bytes 6823936 | tf_op jit(solution)/shard_map/chqk,ckhd->cqhd/dot_general | solution.py:210
  395.9 6.8 convolution_convert_fusion.1
  402.7 16.7 %convert_bitcast_fusion.1 = bf16[8,256,4,128]{1,3,2,0:T(8,128)(2,1)} fusion(f32[8,4,64,256]{3,2,1,0:T(8,128)} %fusion.9, bf16[8,64,4,128]{3,2,1,0:T(4,128)(2,1)S(1)} %reshape.288, f32[8,4,64,256]{3,2,1,0:T(8,128)} %get-tuple-element.50, f32[8,4,64]{2,1,0:T(4,128)S(1)} %get-tuple-element.49), kind=kOutput, calls=%fused_computation.29 | convolution fusion | flops 138938624 | bytes 6823936 | tf_op jit(solution)/shard_map/chqk,cqhd->ckhd/dot_general | solution.py:215
  424.4 7.0 convert_bitcast_fusion
  439.5 4.4 add_convert_fusion
  443.9 5.0 all-to-all-start.4
  448.9 6.7 convolution_convert_fusion.2
  455.7 3.0 convolution_convert_fusion.8
  458.7 3.0 convolution_convert_fusion.9
  461.8 31.0 %all-to-all-done.4 = bf16[4,512,896]{2,1,0:T(8,128)(2,1)} async-done(((bf16[4,512,896]{2,1,0:T(8,128)(2,1)}), bf16[4,512,896]{2,1,0:T(8,128)(2,1)}, u32[]{:S(2)}, u32[]{:S(2)}) %all-to-all-start.4) | async-done | bytes 3670048 | tf_op jit(solution)/shard_map/all_to_all | solution.py:45
  492.8 3.1 reduce_sum.133
  497.9 3.5 all-to-all-start.5
  501.4 4.8 convolution_convert_fusion.3
  511.8 4.9 all-to-all-start.3
  520.1 5.0 reshape_reshape.15
  531.0 5.2 reshape.298
  536.3 6.5 convert_element_type.163
  542.8 36.6 %all-to-all-done.3 = bf16[4,512,1024]{2,1,0:T(8,128)(2,1)} async-done(((bf16[4,512,1024]{2,1,0:T(8,128)(2,1)}), bf16[4,512,1024]{2,1,0:T(8,128)(2,1)}, u32[]{:S(2)}, u32[]{:S(2)}) %all-to-all-start.3) | async-done | bytes 4194336 | tf_op jit(solution)/shard_map/all_to_all | solution.py:45
  579.4 3.5 convert_reduce_fusion
  587.7 58.2 %all-reduce.3.cloned.1.call-done = (bf16[8,4096]{1,0:T(8,128)(2,1)}, bf16[512,4096]{1,0:T(8,128)(2,1)}) async-done(((bf16[8,4096]{1,0:T(8,128)(2,1)}, bf16[512,4096]{1,0:T(8,128)(2,1)}), (bf16[8,4096]{1,0:T(8,128)(2,1)}, bf16[512,4096]{1,0:T(8,128)(2,1)})) %all-reduce.3.cloned.1.call-update) | async-done | bytes 4259856 | tf_op jit(solution)/shard_map/psum | solution.py:263
  645.9 4.9 multiply_reduce_fusion
  651.9 4.0 dynamic-slice_add_fusion
  655.9 75.2 %reduce-scatter.8.cloned.1.call-done = bf16[448,128]{1,0:T(8,128)(2,1)} async-done(((bf16[14336,128]{1,0:T(8,128)(2,1)}), bf16[448,128]{1,0:T(8,128)(2,1)}) %reduce-scatter.8.cloned.1.call-update) | async-done | bytes 114704 | tf_op jit(solution)/shard_map/reduce_scatter | solution.py:55
  (145 shorter events, 63.5 us)
Async XLA Ops:
  7.2 14.6 %copy-start = (bf16[8,128,896]{2,1,0:T(8,128)(2,1)S(1)}, bf16[8,128,896]{2,1,0:T(8,128)(2,1)}, u32[]{:S(2)}) copy-start(bf16[8,128,896]{2,1,0:T(8,128)(2,1)} %param.19) | copy-start | bytes 5505028
  7.2 72.9 %all-gather.9.cloned.1.call-start = ((), (), s32[]{:S(2)}) async-start(), calls=%async_computation.9 | async-start | bytes 5242880 | tf_op jit(solution)/shard_map/all_gather | solution.py:124
  7.9 119.2 %all-gather.11.cloned.1.call-start = ((), (), s32[]{:S(2)}) async-start(), calls=%async_computation.10 | async-start | bytes 1892352 | tf_op jit(solution)/shard_map/all_gather | solution.py:131
  8.7 164.6 %all-gather.21.cloned.1.call-start = ((), (), s32[]{:S(2)}) async-start(), calls=%async_computation.17 | async-start | bytes 2162688 | tf_op jit(solution)/shard_map/all_gather | solution.py:19
  10.2 210.9 %all-gather.15.cloned.1.call-start = ((), (), s32[]{:S(2)}) async-start(), calls=%async_computation.12 | async-start | bytes 4325376 | tf_op jit(solution)/shard_map/all_gather | solution.py:129
  11.6 129.7 %copy-start.19 = (pred[4]{0:T(512)(128)(4,1)}, pred[4]{0:T(512)(128)(4,1)S(1)}, u32[]{:S(2)}) copy-start(pred[4]{0:T(512)(128)(4,1)S(1)} %get-tuple-element.37) | copy-start | bytes 16
  26.9 102.2 %all-to-all-start.1 = ((bf16[4,2,128,896]{3,2,1,0:T(8,128)(2,1)}), bf16[4,2,128,896]{3,2,1,0:T(8,128)(2,1)S(1)}, u32[]{:S(2)}, u32[]{:S(2)}) async-start(bf16[4,2,128,896]{3,2,1,0:T(8,128)(2,1)} %broadcast_select_fusion), calls=%async_computation.1 | async-start | bytes 3670016 | tf_op jit(solution)/shard_map/all_to_all | solution.py:154
  83.1 58.1 %copy-start.13 = (f32[896]{0:T(1024)S(1)}, f32[896]{0:T(1024)}, u32[]{:S(2)}) copy-start(f32[896]{0:T(1024)} %param.18) | copy-start | bytes 10756
  129.2 5.0 copy-start.4
  129.8 9.7 %all-to-all-start.2 = ((bf16[4,8,224]{2,1,0:T(8,128)(2,1)}), bf16[4,8,224]{2,1,0:T(8,128)(2,1)S(1)}, u32[]{:S(2)}, u32[]{:S(2)}) async-start(bf16[4,8,224]{2,1,0:T(8,128)(2,1)} %broadcast_in_dim.82), calls=%async_computation.2 | async-start | bytes 32768 | tf_op jit(solution)/shard_map/all_to_all | solution.py:30
  134.1 132.3 %all-gather.13.cloned.1.call-start = ((), (), s32[]{:S(2)}) async-start(), calls=%async_computation.11 | async-start | bytes 4587520 | tf_op jit(solution)/shard_map/all_gather | solution.py:167
  141.3 35.7 %copy-start.15 = (f32[4,128]{1,0:T(4,128)}, f32[4,128]{1,0:T(4,128)S(1)}, u32[]{:S(2)}) copy-start(f32[4,128]{1,0:T(4,128)S(1)} %get-tuple-element.46) | copy-start | bytes 6148
  142.6 173.8 %all-gather.19.cloned.1.call-start = ((), (), s32[]{:S(2)}) async-start(), calls=%async_computation.14 | async-start | bytes 5242880 | tf_op jit(solution)/shard_map/all_gather | solution.py:192
  143.2 225.1 %all-gather.17.cloned.1.call-start = ((), (), s32[]{:S(2)}) async-start(), calls=%async_computation.13 | async-start | bytes 4325376 | tf_op jit(solution)/shard_map/all_gather | solution.py:134
  144.0 440.3 %reduce-scatter.10.cloned.1.call-start = ((), (), s32[]{:S(2)}) async-start(), calls=%async_computation.18 | async-start | bytes 4325376
  177.0 44.1 %copy-start.17 = (f32[4096]{0:T(1024)S(1)}, f32[4096]{0:T(1024)}, u32[]{:S(2)}) copy-start(f32[4096]{0:T(1024)} %param.12) | copy-start | bytes 49156
  180.6 215.2 %copy-start.22 = (f32[512]{0:T(512)}, f32[512]{0:T(512)S(1)}, u32[]{:S(2)}) copy-start(f32[512]{0:T(512)S(1)} %get-tuple-element.44) | copy-start | bytes 6148
  289.4 2.0 copy-start.2
  329.5 256.6 %reduce-scatter.6.cloned.1.call-start = ((), (), s32[]{:S(2)}) async-start(), calls=%async_computation.15 | async-start | bytes 4325376 | tf_op jit(solution)/shard_map/reduce_scatter | solution.py:224
  434.2 1.6 copy-start.5
  434.2 2.9 copy-start.9
  434.9 4.6 copy-start.7
  443.9 48.9 %all-to-all-start.4 = ((bf16[4,512,896]{2,1,0:T(8,128)(2,1)}), bf16[4,512,896]{2,1,0:T(8,128)(2,1)}, u32[]{:S(2)}, u32[]{:S(2)}) async-start(bf16[4,512,896]{2,1,0:T(8,128)(2,1)} %bitcast.88), calls=%async_computation.4 | async-start | bytes 7340032 | tf_op jit(solution)/shard_map/all_to_all | solution.py:45
  448.9 6.7 copy-start.8
  448.9 6.7 copy-start.25
  455.7 3.0 copy-start.6
  461.7 34.2 %copy-start.14 = (f32[896]{0:T(1024)S(1)}, f32[896]{0:T(1024)}, u32[]{:S(2)}) copy-start(f32[896]{0:T(1024)} %param.18) | copy-start | bytes 10756
  461.7 34.2 %copy-start.20 = (pred[4]{0:T(512)(128)(4,1)S(1)}, pred[4]{0:T(512)(128)(4,1)}, u32[]{:S(2)}) copy-start(pred[4]{0:T(512)(128)(4,1)} %copy-done.19) | copy-start | bytes 16
  461.7 34.7 %copy-start.16 = (f32[4,128]{1,0:T(4,128)S(1)}, f32[4,128]{1,0:T(4,128)}, u32[]{:S(2)}) copy-start(f32[4,128]{1,0:T(4,128)} %copy-done.15) | copy-start | bytes 6148
  461.8 34.7 %copy-start.24 = (f32[4,128]{1,0:T(4,128)S(1)}, f32[4,128]{1,0:T(4,128)}, u32[]{:S(2)}) copy-start(f32[4,128]{1,0:T(4,128)} %get-tuple-element.45) | copy-start | bytes 6148
  497.9 13.9 %all-to-all-start.5 = ((f32[4,4,896]{2,1,0:T(4,128)}), f32[4,4,896]{2,1,0:T(4,128)S(1)}, u32[]{:S(2)}, u32[]{:S(2)}) async-start(f32[4,4,896]{2,1,0:T(4,128)} %broadcast_in_dim.84), calls=%async_computation.5 | async-start | bytes 114688 | tf_op jit(solution)/shard_map/all_to_all | solution.py:30
  506.2 2.4 copy-start.11
  508.6 1.2 copy-start.10
  511.8 67.6 %all-to-all-start.3 = ((bf16[4,512,1024]{2,1,0:T(8,128)(2,1)}), bf16[4,512,1024]{2,1,0:T(8,128)(2,1)}, u32[]{:S(2)}, u32[]{:S(2)}) async-start(bf16[4,512,1024]{2,1,0:T(8,128)(2,1)} %bitcast.80), calls=%async_computation.3 | async-start | bytes 8388608 | tf_op jit(solution)/shard_map/all_to_all | solution.py:45
  516.7 129.2 %all-reduce.3.cloned.1.call-start = ((), (), s32[]{:S(2)}) async-start(), calls=%async_computation.19 | async-start | bytes 8519680 | tf_op jit(solution)/shard_map/psum | solution.py:263
  527.7 203.4 %reduce-scatter.8.cloned.1.call-start = ((), (), s32[]{:S(2)}) async-start(), calls=%async_computation.16 | async-start | bytes 3784704 | tf_op jit(solution)/shard_map/reduce_scatter | solution.py:55
  542.8 40.1 %copy-start.3 = (bf16[512,1024]{1,0:T(8,128)(2,1)S(1)}, bf16[512,1024]{1,0:T(8,128)(2,1)}, u32[]{:S(2)}) copy-start(bf16[512,1024]{1,0:T(8,128)(2,1)} %param.11) | copy-start | bytes 3145732
  582.9 63.0 %copy-start.18 = (f32[4096]{0:T(1024)S(1)}, f32[4096]{0:T(1024)}, u32[]{:S(2)}) copy-start(f32[4096]{0:T(1024)} %param.12) | copy-start | bytes 49156
  645.9 4.9 copy-start.12
  650.9 1.0 copy-start.21
  650.9 1.0 copy-start.23
  651.9 83.0 %copy-start.1 = (bf16[8,128,896]{2,1,0:T(8,128)(2,1)S(1)}, bf16[8,128,896]{2,1,0:T(8,128)(2,1)}, u32[]{:S(2)}) copy-start(bf16[8,128,896]{2,1,0:T(8,128)(2,1)} %param.19) | copy-start | bytes 5505028
Sparse Core Ops, SparseCore 0:
  9.7 70.3 all-gather.8
  82.3 44.7 all-gather.10
  129.9 43.2 all-gather.20
  175.4 45.6 all-gather.14
  223.1 43.2 all-gather.12
  267.9 48.4 all-gather.18
  318.6 49.7 all-gather.16
  372.0 81.5 reduce-scatter.9
  457.7 81.2 reduce-scatter.5
  541.9 103.9 all-reduce.2
  650.0 81.0 reduce-scatter.7
where the time goes:
time: 752 us; the launch traced here: 742 us
  waiting for transfers between devices  467 us (62%)
  matrix products  119 us (16%)
  local copies, waits for them, and re-layouts  60.3 us (8%)
  other arithmetic  48.4 us (6%)
  starting transfers between devices  22.4 us (3%)
  between operations  14.9 us (2%)
  blocking collectives  9.59 us (1%)
    reduce_scatter x1, waiting for transfers between devices, one_scatter(): lax.psum_scatter(lines, axis, tiled=True).reshape(-1)  75.2 us
    all_to_all x2, waiting for transfers between devices, summed_on_arrival(): tiles = lax.all_to_all(in_blocks(shard, dim, peers), axis, 0, 0, tiled=True)  67.6 us
    psum x1, waiting for transfers between devices, shards(): lax.psum(summary_term.astype(jnp.bfloat16), 'enc').astype(jnp.float32)  58.2 us
    all_gather x1, waiting for transfers between devices, shards(): full_rows = lax.all_gather(hidden, 'enc', axis=1, tiled=True)  49.5 us
    all_gather x1, waiting for transfers between devices, shards(): lax.all_gather(w_cond, 'dp', axis=0, tiled=True)  43.9 us
    all_gather x1, waiting for transfers between devices, shards(): lax.all_gather(w_query, 'dp', axis=0, tiled=True)  40.4 us
    all_gather x1, waiting for transfers between devices, shards(): encoded = lax.all_gather(encoded_mine, 'enc', axis=0, tiled=True)  39.4 us
    all_gather x1, waiting for transfers between devices, shards(): w_out_all = lax.all_gather(w_out, 'dp', axis=1, tiled=True)  38.4 us
  transfers between devices with their start and end apart: 16, of which 12 were waited for; matrix products, arithmetic and copies ran while one was open for 30% of the time, Pallas kernels for 0%

commit v1 on v0

--- a/solution.py
+++ b/solution.py
@@ -8,6 +8,17 @@
 NBR = 2
 NL = 128
 epsilon = 1e-05
+
+
+def pass_along(array, name, d):
+    devices = lax.axis_size(name)
+    forward = [(i, (i + 1) % devices) for i in range(devices)]
+    parts = [array]
+    for far in range(1, devices):
+        parts = [lax.ppermute(parts[0], name, forward), *parts]
+    whole = jnp.concatenate(parts, axis=d)
+    shift = (lax.axis_index(name) + 1) * parts[-1].shape[d]
+    return jnp.roll(whole, shift, axis=d)
 
 
 def side_by_side(arrays, axis, dim, along):
@@ -121,7 +132,7 @@
     heads_here = head_cols // HSZ
     keys_len = NBR * NL
     score_scale = HSZ ** (-0.5)
-    full_rows = lax.all_gather(hidden, "enc", axis=1, tiled=True)
+    full_rows = pass_along(hidden, "enc", 1)
     inputs = full_rows.astype(jnp.float32)
     row_rstd = rms_scale(inputs)
     normed = (inputs * row_rstd * norm_gain).astype(jnp.bfloat16)

time: 752 us -> 685 us (0.911)
  waiting for transfers between devices: 467 us -> 390 us
  local copies, waits for them, and re-layouts: 60.3 us -> 75.3 us
  blocking collectives: 9.59 us -> 0 us
    ppermute x0 -> x3, waiting for transfers between devices: none -> 61.9 us  [pass_along(): parts = [lax.ppermute(parts[0], name, forward), *parts]]
    all_gather x1 -> x0, waiting for transfers between devices: 49.5 us -> none  [shards(): full_rows = lax.all_gather(hidden, 'enc', axis=1, tiled=True)]
    all_gather x1, waiting for transfers between devices: 43.9 us -> 0.02 us  [shards(): lax.all_gather(w_cond, 'dp', axis=0, tiled=True)]
    all_gather x1, waiting for transfers between devices: 29.2 us -> 0.01 us  [side_by_side(): lax.all_gather(both, axis, axis=dim, tiled=True)]
    all_gather x1, waiting for transfers between devices: 40.4 us -> 23.4 us  [shards(): lax.all_gather(w_query, 'dp', axis=0, tiled=True)]
    unnamed x58 -> x67, local copies, waits for them, and re-layouts: 17.1 us -> 26.7 us
    all_to_all x1 -> x0, blocking collectives: 9.59 us -> none  [shards(): lax.all_to_all(row_buffer, 'enc', split_axis=0, concat_axis=0, tiled=True)]
  transfers between devices with their start and end apart: 16 -> 19, of which waited for: 12 -> 13; matrix products, arithmetic and copies ran while one was open for 30% -> 34% of each run, Pallas kernels for 0% -> 0%
where the time goes in v1:
time: 685 us; the launch traced here: 679 us
  waiting for transfers between devices  390 us (57%)
  matrix products  121 us (18%)
  local copies, waits for them, and re-layouts  75.3 us (11%)
  other arithmetic  47.9 us (7%)
  starting transfers between devices  29.4 us (4%)
  between operations  15.2 us (2%)
    reduce_scatter x1, waiting for transfers between devices, one_scatter(): lax.psum_scatter(lines, axis, tiled=True).reshape(-1)  75.1 us
    all_to_all x2, waiting for transfers between devices, summed_on_arrival(): tiles = lax.all_to_all(in_blocks(shard, dim, peers), axis, 0, 0, tiled=True)  72.8 us
    ppermute x3, waiting for transfers between devices, pass_along(): parts = [lax.ppermute(parts[0], name, forward), *parts]  61.9 us
    psum x1, waiting for transfers between devices, shards(): lax.psum(summary_term.astype(jnp.bfloat16), 'enc').astype(jnp.float32)  52.2 us
    all_gather x1, waiting for transfers between devices, shards(): encoded = lax.all_gather(encoded_mine, 'enc', axis=0, tiled=True)  39.4 us
    all_gather x1, waiting for transfers between devices, shards(): w_out_all = lax.all_gather(w_out, 'dp', axis=1, tiled=True)  38.2 us
    unnamed x67, local copies, waits for them, and re-layouts  26.7 us
    all_gather x1, waiting for transfers between devices, shards(): lax.all_gather(w_query, 'dp', axis=0, tiled=True)  23.4 us
  transfers between devices with their start and end apart: 19, of which 13 were waited for; matrix products, arithmetic and copies ran while one was open for 34% of the time, Pallas kernels for 0%

profile of v1, /device:TPU:0, one launch (start us, length us, event | category | flops | bytes accessed | tf_op | source)
XLA Modules:
  0.0 678.6 jit_solution(17137030095943042444)
XLA Ops:
  11.9 24.8 %collective-permute-done = bf16[512,1024]{1,0:T(8,128)(2,1)S(1)} collective-permute-done((bf16[512,1024]{1,0:T(8,128)(2,1)}, bf16[512,1024]{1,0:T(8,128)(2,1)S(1)}, u32[]{:S(2)}, u32[]{:S(2)}) %collective-permute-start) | collective-permute-done | bytes 1048608 | tf_op jit(solution)/shard_map/ppermute | solution.py:18
  38.6 4.2 all-to-all-start
  42.8 19.4 %collective-permute-done.1 = bf16[512,1024]{1,0:T(8,128)(2,1)} collective-permute-done((bf16[512,1024]{1,0:T(8,128)(2,1)S(1)}, bf16[512,1024]{1,0:T(8,128)(2,1)}, u32[]{:S(2)}, u32[]{:S(2)}) %collective-permute-start.1) | collective-permute-done | bytes 1048608 | tf_op jit(solution)/shard_map/ppermute | solution.py:18
  67.6 4.5 all-to-all-start.1
  72.1 17.7 %collective-permute-done.2 = bf16[512,1024]{1,0:T(8,128)(2,1)} collective-permute-done((bf16[512,1024]{1,0:T(8,128)(2,1)}, bf16[512,1024]{1,0:T(8,128)(2,1)}, u32[]{:S(2)}, u32[]{:S(2)}) %collective-permute-start.2) | collective-permute-done | bytes 1048608 | tf_op jit(solution)/shard_map/ppermute | solution.py:18
  95.7 3.2 copy-done.2
  101.9 4.7 all-to-all-done.1
  107.3 3.3 all-to-all-start.2
  112.8 3.0 all-to-all-done.2
  120.4 3.1 multiply_reduce_fusion.1
  124.1 3.7 reshape.330
  127.8 23.4 %all-gather.12.cloned.1.call-done = bf16[4096,512]{1,0:T(8,128)(2,1)} async-done(((bf16[128,512]{1,0:T(8,128)(2,1)}), bf16[4096,512]{1,0:T(8,128)(2,1)}) %all-gather.12.cloned.1.call-update) | async-done | bytes 4194320 | tf_op jit(solution)/shard_map/all_gather | solution.py:140
  151.2 5.8 convolution_convert_fusion.11
  157.2 39.4 %all-gather.10.cloned.1.call-done = bf16[16,128,896]{2,1,0:T(8,128)(2,1)} async-done(((bf16[4,128,896]{2,1,0:T(8,128)(2,1)}), bf16[16,128,896]{2,1,0:T(8,128)(2,1)}) %all-gather.10.cloned.1.call-update) | async-done | bytes 3670032 | tf_op jit(solution)/shard_map/all_gather | solution.py:178
  196.6 5.9 convolution_convert_fusion.6
  202.5 4.0 reshape.289
  206.5 6.4 convolution_convert_fusion.7
  212.9 4.2 reshape.287
  221.6 6.8 fusion.34
  229.8 16.8 %all-gather.16.cloned.1.call-done = bf16[512,4096]{1,0:T(8,128)(2,1)} async-done(((bf16[512,1024]{1,0:T(8,128)(2,1)}), bf16[512,4096]{1,0:T(8,128)(2,1)}) %all-gather.16.cloned.1.call-update) | async-done | bytes 4194320 | tf_op jit(solution)/shard_map/all_gather | solution.py:203
  246.6 6.5 convolution_convert_fusion
  253.1 6.5 copy.112
  260.2 38.2 %all-gather.14.cloned.1.call-done = bf16[512,4096]{1,0:T(8,128)(2,1)} async-done(((bf16[512,128]{1,0:T(8,128)(2,1)}), bf16[512,4096]{1,0:T(8,128)(2,1)}) %all-gather.14.cloned.1.call-update) | async-done | bytes 4194320 | tf_op jit(solution)/shard_map/all_gather | solution.py:145
  298.4 6.6 convolution_convert_fusion.10
  307.0 3.9 fusion.9
  310.9 16.3 %fusion.37 = bf16[8,64,4,128]{3,1,2,0:T(8,128)(2,1)} fusion(bf16[8,256,4,128]{3,2,1,0:T(4,128)(2,1)} %reshape.289, f32[8,4,64,256]{3,2,1,0:T(8,128)} %fusion.9, f32[8,4,64,256]{3,2,1,0:T(8,128)} %get-tuple-element.50, f32[8,4,64]{2,1,0:T(4,128)S(1)} %get-tuple-element.49), kind=kOutput, calls=%fused_computation.63 | convolution fusion | flops 138152192 | bytes 6823936 | tf_op jit(solution)/shard_map/chqk,ckhd->cqhd/dot_general | solution.py:221
  329.5 6.8 %convolution_convert_fusion.1 = bf16[4096,512]{1,0:T(8,128)(2,1)} fusion(f32[4096]{0:T(1024)S(1)} %copy-done.20, f32[512]{0:T(512)S(1)} %get-tuple-element.44, bf16[512,8192]{1,0:T(8,128)(2,1)} %copy-done.2, s32[]{:T(128)S(6)} %select_n.119, bf16[64,8,4,128]{3,2,1,0:T(4,128)(2,1)S(1)} %bitcast.94), kind=kOutput, calls=%fused_computation.13 | convolution fusion | flops 2157969408 | bytes 8931332 | tf_op jit(solution)/shard_map/dot_general | solution.py:96
  336.4 16.5 %convert_bitcast_fusion.1 = bf16[8,256,4,128]{1,3,2,0:T(8,128)(2,1)} fusion(f32[8,4,64,256]{3,2,1,0:T(8,128)} %fusion.9, bf16[8,64,4,128]{3,2,1,0:T(4,128)(2,1)S(1)} %reshape.288, f32[8,4,64,256]{3,2,1,0:T(8,128)} %get-tuple-element.50, f32[8,4,64]{2,1,0:T(4,128)S(1)} %get-tuple-element.49), kind=kOutput, calls=%fused_computation.30 | convolution fusion | flops 138938624 | bytes 6823936 | tf_op jit(solution)/shard_map/chqk,cqhd->ckhd/dot_general | solution.py:226
  357.9 7.0 %convert_bitcast_fusion = bf16[8,256,4,128]{1,3,2,0:T(8,128)(2,1)} fusion(bf16[8,64,4,128]{3,2,1,0:T(4,128)(2,1)S(1)} %copy-done.7, f32[8,4,64]{2,1,0:T(4,128)S(1)} %get-tuple-element.49, f32[8,4,64,256]{3,2,1,0:T(8,128)} %copy-done.4), kind=kOutput, calls=%fused_computation.29 | convolution fusion | flops 137365760 | bytes 4726784 | tf_op jit(solution)/shard_map/chqk,cqhd->ckhd/dot_general | solution.py:231
  373.0 4.4 add_convert_fusion
  377.4 5.1 all-to-all-start.4
  382.5 6.7 convolution_convert_fusion.2
  389.3 3.0 convolution_convert_fusion.8
  395.3 31.1 %all-to-all-done.4 = bf16[4,512,896]{2,1,0:T(8,128)(2,1)} async-done(((bf16[4,512,896]{2,1,0:T(8,128)(2,1)}), bf16[4,512,896]{2,1,0:T(8,128)(2,1)}, u32[]{:S(2)}, u32[]{:S(2)}) %all-to-all-start.4) | async-done | bytes 3670048 | tf_op jit(solution)/shard_map/all_to_all | solution.py:56
  426.5 3.1 reduce_sum.133
  432.9 4.1 all-to-all-start.5
  437.0 4.6 convolution_convert_fusion.3
  448.0 4.8 all-to-all-start.3
  457.1 5.0 reshape_reshape.15
  465.0 3.1 pad_maximum_fusion
  468.1 5.3 reshape.298
  473.5 6.8 %dynamic-slice_convert_fusion = f32[512,4096]{1,0:T(8,128)} fusion(bf16[512,8192]{1,0:T(8,128)(2,1)} %copy-done.2, s32[]{:T(128)S(6)} %select_n.119), kind=kLoop, calls=%fused_computation.22 | loop fusion | flops 2097152 | bytes 12582916 | tf_op jit(solution)/shard_map/convert_element_type | solution.py:136
  480.3 41.6 %all-to-all-done.3 = bf16[4,512,1024]{2,1,0:T(8,128)(2,1)} async-done(((bf16[4,512,1024]{2,1,0:T(8,128)(2,1)}), bf16[4,512,1024]{2,1,0:T(8,128)(2,1)}, u32[]{:S(2)}, u32[]{:S(2)}) %all-to-all-start.3) | async-done | bytes 4194336 | tf_op jit(solution)/shard_map/all_to_all | solution.py:56
  521.9 3.5 convert_reduce_fusion
  530.2 52.2 %all-reduce.3.cloned.1.call-done = (bf16[8,4096]{1,0:T(8,128)(2,1)}, bf16[512,4096]{1,0:T(8,128)(2,1)}) async-done(((bf16[8,4096]{1,0:T(8,128)(2,1)}, bf16[512,4096]{1,0:T(8,128)(2,1)}), (bf16[8,4096]{1,0:T(8,128)(2,1)}, bf16[512,4096]{1,0:T(8,128)(2,1)})) %all-reduce.3.cloned.1.call-update) | async-done | bytes 4259856 | tf_op jit(solution)/shard_map/psum | solution.py:274
  582.4 4.9 multiply_reduce_fusion
  588.4 4.0 dynamic-slice_add_fusion
  592.4 75.1 %reduce-scatter.8.cloned.1.call-done = bf16[448,128]{1,0:T(8,128)(2,1)} async-done(((bf16[14336,128]{1,0:T(8,128)(2,1)}), bf16[448,128]{1,0:T(8,128)(2,1)}) %reduce-scatter.8.cloned.1.call-update) | async-done | bytes 114704 | tf_op jit(solution)/shard_map/reduce_scatter | solution.py:66
  (158 shorter events, 82.0 us)
Async XLA Ops:
  7.2 55.5 %copy-start = (bf16[8,128,896]{2,1,0:T(8,128)(2,1)S(1)}, bf16[8,128,896]{2,1,0:T(8,128)(2,1)}, u32[]{:S(2)}) copy-start(bf16[8,128,896]{2,1,0:T(8,128)(2,1)} %param.19) | copy-start | bytes 5505028
  7.2 92.7 %all-gather.8.cloned.1.call-start = ((), (), s32[]{:S(2)}) async-start(), calls=%async_computation.9 | async-start | bytes 1892352 | tf_op jit(solution)/shard_map/all_gather | solution.py:142
  7.9 116.2 %all-gather.18.cloned.1.call-start = ((), (), s32[]{:S(2)}) async-start(), calls=%async_computation.16 | async-start | bytes 2162688 | tf_op jit(solution)/shard_map/all_gather | solution.py:30
  9.4 141.8 %all-gather.12.cloned.1.call-start = ((), (), s32[]{:S(2)}) async-start(), calls=%async_computation.11 | async-start | bytes 4325376 | tf_op jit(solution)/shard_map/all_gather | solution.py:140
  10.1 26.5 %collective-permute-start = (bf16[512,1024]{1,0:T(8,128)(2,1)}, bf16[512,1024]{1,0:T(8,128)(2,1)S(1)}, u32[]{:S(2)}, u32[]{:S(2)}) collective-permute-start(bf16[512,1024]{1,0:T(8,128)(2,1)} %param.11), channel_id=1, source_target_pairs={{0,1},{1,2},{2,3},{3,0},{4,5},{5,6},{6,7},{7,4},{8,9},{9,10},{10,1... | collective-permute-start | bytes 3145736 | tf_op jit(solution)/shard_map/ppermute | solution.py:18
  36.7 31.0 %copy-start.5 = (bf16[512,1024]{1,0:T(8,128)(2,1)}, bf16[512,1024]{1,0:T(8,128)(2,1)S(1)}, u32[]{:S(2)}) copy-start(bf16[512,1024]{1,0:T(8,128)(2,1)S(1)} %collective-permute-done) | copy-start | bytes 3145732
  36.7 25.5 %collective-permute-start.1 = (bf16[512,1024]{1,0:T(8,128)(2,1)S(1)}, bf16[512,1024]{1,0:T(8,128)(2,1)}, u32[]{:S(2)}, u32[]{:S(2)}) collective-permute-start(bf16[512,1024]{1,0:T(8,128)(2,1)S(1)} %collective-permute-done), channel_id=1, source_target_pairs={{0,1},{1,2},{2,3},{3,0},{4,5},{5,6},{6,7},{7,4},{8,9},{9,10},{10,1... | collective-permute-start | bytes 3145736 | tf_op jit(solution)/shard_map/ppermute | solution.py:18
  37.9 79.8 %copy-start.22 = (pred[4]{0:T(512)(128)(4,1)}, pred[4]{0:T(512)(128)(4,1)S(1)}, u32[]{:S(2)}) copy-start(pred[4]{0:T(512)(128)(4,1)S(1)} %get-tuple-element.37) | copy-start | bytes 16
  38.6 23.6 %all-to-all-start = ((s32[4,1,2]{2,1,0:T(1,128)}), s32[4,1,2]{2,1,0:T(1,128)S(1)}, u32[]{:S(2)}, u32[]{:S(2)}) async-start(s32[4,1,2]{2,1,0:T(1,128)} %bitcast), calls=%async_computation | async-start | bytes 4096 | tf_op jit(solution)/shard_map/all_to_all | solution.py:168
  62.2 27.6 %collective-permute-start.2 = (bf16[512,1024]{1,0:T(8,128)(2,1)}, bf16[512,1024]{1,0:T(8,128)(2,1)}, u32[]{:S(2)}, u32[]{:S(2)}) collective-permute-start(bf16[512,1024]{1,0:T(8,128)(2,1)} %collective-permute-done.1), channel_id=1, source_target_pairs={{0,1},{1,2},{2,3},{3,0},{4,5},{5,6},{6,7},{7,4},{8,9},{9,10},{10,1... | collective-permute-start | bytes 3145736 | tf_op jit(solution)/shard_map/ppermute | solution.py:18
  67.6 39.0 %all-to-all-start.1 = ((bf16[4,2,128,896]{3,2,1,0:T(8,128)(2,1)}), bf16[4,2,128,896]{3,2,1,0:T(8,128)(2,1)}, u32[]{:S(2)}, u32[]{:S(2)}) async-start(bf16[4,2,128,896]{3,2,1,0:T(8,128)(2,1)} %broadcast_select_fusion), calls=%async_computation.1 | async-start | bytes 3670016 | tf_op jit(solution)/shard_map/all_to_all | solution.py:165
  72.1 20.4 %copy-start.6 = (bf16[512,1024]{1,0:T(8,128)(2,1)S(1)}, bf16[512,1024]{1,0:T(8,128)(2,1)}, u32[]{:S(2)}) copy-start(bf16[512,1024]{1,0:T(8,128)(2,1)} %copy-done.5) | copy-start | bytes 3145732
  91.2 1.5 copy-start.3
  95.7 3.2 copy-start.2
  99.8 17.8 %copy-start.18 = (f32[896]{0:T(1024)S(1)}, f32[896]{0:T(1024)}, u32[]{:S(2)}) copy-start(f32[896]{0:T(1024)} %param.18) | copy-start | bytes 10756
  107.3 8.6 %all-to-all-start.2 = ((bf16[4,8,224]{2,1,0:T(8,128)(2,1)}), bf16[4,8,224]{2,1,0:T(8,128)(2,1)S(1)}, u32[]{:S(2)}, u32[]{:S(2)}) async-start(bf16[4,8,224]{2,1,0:T(8,128)(2,1)} %broadcast_in_dim.82), calls=%async_computation.2 | async-start | bytes 32768 | tf_op jit(solution)/shard_map/all_to_all | solution.py:41
  110.5 86.0 %all-gather.10.cloned.1.call-start = ((), (), s32[]{:S(2)}) async-start(), calls=%async_computation.10 | async-start | bytes 4587520 | tf_op jit(solution)/shard_map/all_gather | solution.py:178
  117.6 5.9 copy-start.19
  119.0 127.6 %all-gather.16.cloned.1.call-start = ((), (), s32[]{:S(2)}) async-start(), calls=%async_computation.13 | async-start | bytes 5242880 | tf_op jit(solution)/shard_map/all_gather | solution.py:203
  119.6 178.8 %all-gather.14.cloned.1.call-start = ((), (), s32[]{:S(2)}) async-start(), calls=%async_computation.12 | async-start | bytes 4325376 | tf_op jit(solution)/shard_map/all_gather | solution.py:145
  120.2 406.6 %reduce-scatter.10.cloned.1.call-start = ((), (), s32[]{:S(2)}) async-start(), calls=%async_computation.17 | async-start | bytes 4325376
  123.5 27.7 %copy-start.20 = (f32[4096]{0:T(1024)S(1)}, f32[4096]{0:T(1024)}, u32[]{:S(2)}) copy-start(f32[4096]{0:T(1024)} %param.12) | copy-start | bytes 49156
  124.1 204.6 %copy-start.24 = (f32[512]{0:T(512)}, f32[512]{0:T(512)S(1)}, u32[]{:S(2)}) copy-start(f32[512]{0:T(512)S(1)} %get-tuple-element.44) | copy-start | bytes 6148
  219.6 2.0 copy-start.4
  259.7 268.8 %reduce-scatter.6.cloned.1.call-start = ((), (), s32[]{:S(2)}) async-start(), calls=%async_computation.14 | async-start | bytes 4325376 | tf_op jit(solution)/shard_map/reduce_scatter | solution.py:235
  328.7 0.8 copy-start.15
  355.9 2.0 copy-start.7
  367.7 1.6 copy-start.8
  367.7 2.9 copy-start.12
  368.4 4.6 copy-start.10
  377.4 5.1 copy-start.16
  377.4 49.1 %all-to-all-start.4 = ((bf16[4,512,896]{2,1,0:T(8,128)(2,1)}), bf16[4,512,896]{2,1,0:T(8,128)(2,1)}, u32[]{:S(2)}, u32[]{:S(2)}) async-start(bf16[4,512,896]{2,1,0:T(8,128)(2,1)} %bitcast.87), calls=%async_computation.4 | async-start | bytes 7340032 | tf_op jit(solution)/shard_map/all_to_all | solution.py:56
  382.5 6.7 copy-start.11
  382.5 6.7 copy-start.26
  389.3 3.0 copy-start.9
  432.9 15.2 %all-to-all-start.5 = ((f32[4,4,896]{2,1,0:T(4,128)}), f32[4,4,896]{2,1,0:T(4,128)}, u32[]{:S(2)}, u32[]{:S(2)}) async-start(f32[4,4,896]{2,1,0:T(4,128)} %broadcast_in_dim.84), calls=%async_computation.5 | async-start | bytes 114688 | tf_op jit(solution)/shard_map/all_to_all | solution.py:41
  441.6 2.4 copy-start.14
  444.0 2.0 copy-start.13
  448.0 73.9 %all-to-all-start.3 = ((bf16[4,512,1024]{2,1,0:T(8,128)(2,1)}), bf16[4,512,1024]{2,1,0:T(8,128)(2,1)}, u32[]{:S(2)}, u32[]{:S(2)}) async-start(bf16[4,512,1024]{2,1,0:T(8,128)(2,1)} %bitcast.80), calls=%async_computation.3 | async-start | bytes 8388608 | tf_op jit(solution)/shard_map/all_to_all | solution.py:56
  452.9 129.5 %all-reduce.3.cloned.1.call-start = ((), (), s32[]{:S(2)}) async-start(), calls=%async_computation.18 | async-start | bytes 8519680 | tf_op jit(solution)/shard_map/psum | solution.py:274
  464.7 202.8 %reduce-scatter.8.cloned.1.call-start = ((), (), s32[]{:S(2)}) async-start(), calls=%async_computation.15 | async-start | bytes 3784704 | tf_op jit(solution)/shard_map/reduce_scatter | solution.py:66
  525.4 57.0 %copy-start.21 = (f32[4096]{0:T(1024)S(1)}, f32[4096]{0:T(1024)}, u32[]{:S(2)}) copy-start(f32[4096]{0:T(1024)} %param.12) | copy-start | bytes 49156
  582.4 4.9 copy-start.17
  587.4 1.0 copy-start.23
  587.4 1.0 copy-start.25
  588.4 82.8 %copy-start.1 = (bf16[8,128,896]{2,1,0:T(8,128)(2,1)S(1)}, bf16[8,128,896]{2,1,0:T(8,128)(2,1)}, u32[]{:S(2)}) copy-start(bf16[8,128,896]{2,1,0:T(8,128)(2,1)} %param.19) | copy-start | bytes 5505028
Sparse Core Ops, SparseCore 0:
  10.2 46.8 all-gather.7
  60.0 43.1 all-gather.17
  105.5 45.7 all-gather.11
  153.3 43.2 all-gather.9
  198.1 48.4 all-gather.15
  248.6 49.7 all-gather.13
  302.0 81.5 reduce-scatter.9
  387.7 81.2 reduce-scatter.5
  472.1 110.3 all-reduce.2
  586.4 81.0 reduce-scatter.7
